TPU v7x, 32 devices: a whole 2x2x4 slice. The times are simulated.
32 devices in a mesh: groups: 2 (over x), expert: 16 (over z, y, core).
Axes of the slice: x: 2, y: 2, z: 4, core: 2. Of those that a mesh axis runs over, the one named last changes fastest.
Arguments:
- hidden_states: bfloat16 [2, 1024, 2560], P(None, ('groups', 'expert')), parts along dimension 1, may hold values from -6 to 6
- route_ids: int32 [2, 1024, 8], P(None, ('groups', 'expert')), parts along dimension 1, may hold values from 0 to 15, all different within a row; in each aligned block of 32 rows (0 to 31, 32 to 63, ..., all dimensions but the last counted through in order) at most 24 rows name the same one
- route_weights: float32 [2, 1024, 8], P(None, ('groups', 'expert')), parts along dimension 1, may hold values from 0.05 to 1
- gate_proj: bfloat16 [16, 2560, 768], P('expert'), may hold values from -0.125 to 0.125
- up_proj: bfloat16 [16, 2560, 768], P('expert'), may hold values from -0.125 to 0.125
- down_proj: bfloat16 [16, 768, 2560], P('expert'), may hold values from -0.21875 to 0.21875
Outputs:
- moe_output: bfloat16 [2, 1024, 2560], P(None, ('groups', 'expert')), parts along dimension 1
There are 2 independent parts, one for each index of `groups`. A program takes and returns all parts, laid end to end along the dimension named above; an argument that names none is the same for every part. Nothing has to cross between parts.
Inputs may be any that keep to these rules, and one draw needn't show every extreme that they name: `route_ids`: each row names 8 different experts. In each micro-batch, the 32 rows of one device name one expert at most 24 times, and some device names some expert exactly 24 times.
All inputs are finite; a program needn't handle non-finite values.
Results may differ from a plain program's by a relative error of at most 0.0057.
Values may be sent and summed in bfloat16 or wider, within the bound.
A program may use at most 64 MiB of HBM per device.

v0:
```python
import functools

import jax
import jax.numpy as jnp
from jax import lax
from jax.experimental import pallas as pl
from jax.experimental.pallas import tpu as pltpu
from jax.sharding import PartitionSpec as P

MESH = pl.DeviceIdType.MESH
LANES = 128
CUTS = 2


def kernel(
    chips,
    across,
    hidden_ref,
    ids_ref,
    weights_ref,
    gate_hbm,
    up_hbm,
    down_hbm,
    out_ref,
    x,
    pc,
    rs,
    gate,
    up,
    down,
    mid,
    load_sem,
    ag_s,
    ag_r,
    pf_s,
    pf_r,
    pc_s,
    pc_r,
    rs_s,
    rs_r,
):
    steps, _, _, rows, _ = x.shape
    width = out_ref.shape[2]
    inner = gate.shape[1]
    experts = 2 * chips
    hops = (chips // 2, chips - 1 - chips // 2)
    along = chips // across

    me = lax.axis_index("expert")
    core = lax.rem(me, 2)
    chip = lax.div(me, 2)
    if across == 2:
        far, deep = lax.rem(chip, 2), lax.div(chip, 2)
        here = (1 - far) * deep + far * (2 * along - 1 - deep)
    else:
        here = chip

    def device_at(position):
        if across == 2:
            far = lax.div(position, along)
            deep = (1 - far) * position + far * (2 * along - 1 - position)
            position = deep * 2 + far
        return {"expert": position * 2 + core}

    sign = 1 - 2 * core
    neighbours = (
        device_at(lax.rem(here + sign + chips, chips)),
        device_at(lax.rem(here - sign + chips, chips)),
    )
    partner = {"expert": chip * 2 + (1 - core)}

    def slot(direction, hop):
        return hop if direction == 0 else (chips - hop) % chips

    order = [0]
    for hop in range(1, chips // 2 + 1):
        order += [slot(d, hop) for d in range(2) if hop <= hops[d]]
    place = {s: i for i, s in enumerate(order)}
    values = pl.ds(0, width)
    cut = rows // CUTS

    def some(q):
        return pl.ds(q * cut, cut)

    def remote(src, dst, send, recv, target):
        return pltpu.make_async_remote_copy(
            src_ref=src,
            dst_ref=dst,
            send_sem=send,
            recv_sem=recv,
            device_id=target,
            device_id_type=MESH,
        )

    def mirror(s):
        return (chips - s) % chips

    def ag_copy(st, d, hop, q):
        return remote(
            x.at[st, place[slot(d, hop - 1)], 0, some(q)],
            x.at[st, place[slot(d, hop)], 0, some(q)],
            ag_s.at[st, d, hop - 1, q],
            ag_r.at[st, d, hop - 1, q],
            neighbours[d],
        )

    def pf_copy(st, s, q):
        return remote(
            x.at[st, place[s], 0, some(q)],
            x.at[st, place[mirror(s)], 1, some(q)],
            pf_s.at[st, s, q],
            pf_r.at[st, mirror(s), q],
            partner,
        )

    def pc_copy(st, s):
        return remote(
            x.at[st, place[s], 1, :, values],
            pc.at[st, mirror(s)],
            pc_s.at[st, s],
            pc_r.at[st, mirror(s)],
            partner,
        )

    def rs_copy(st, d, hop, q):
        target = slot(d, hop - 1) if (d == 0 or hop > 1) else chips // 2
        return remote(
            x.at[st, place[slot(d, hop)], 0, some(q), values],
            rs.at[st, target, some(q)],
            rs_s.at[st, d, hop - 1, q],
            rs_r.at[st, d, hop - 1, q],
            neighbours[1 - d],
        )

    barrier = pltpu.get_barrier_semaphore()
    for target in (*neighbours, partner):
        pl.semaphore_signal(barrier, inc=1, device_id=target, device_id_type=MESH)

    own = [
        pltpu.make_async_copy(
            hidden_ref.at[st], x.at[st, 0, 0, :, values], load_sem.at[3 + st]
        )
        for st in range(steps)
    ]
    for copy in own:
        copy.start()
    loads = [
        pltpu.make_async_copy(src.at[0], dst, load_sem.at[i])
        for i, (src, dst) in enumerate(((gate_hbm, gate), (up_hbm, up), (down_hbm, down)))
    ]
    for copy in loads:
        copy.start()

    extra = x.shape[4] - width
    lane = lax.broadcasted_iota(jnp.int32, (rows, extra), 1)
    for st in range(steps):
        raw = weights_ref[st]
        normalized = (raw / jnp.sum(raw, axis=0, keepdims=True)).T
        ids = ids_ref[st].T
        dense = jnp.zeros((rows, extra), jnp.float32)
        for k in range(ids.shape[1]):
            label = ids[:, k : k + 1]
            hit = (lane == label) | (lane == label + experts)
            dense = dense + jnp.where(hit, normalized[:, k : k + 1], 0.0)
        high = dense.astype(jnp.bfloat16).astype(jnp.float32)
        low = dense - high
        x[st, 0, 0, :, pl.ds(width, extra)] = jnp.where(lane < experts, high, low).astype(
            jnp.bfloat16
        )
    pl.semaphore_wait(barrier, 3)

    def ag_open(st):
        own[st].wait()
        for q in range(CUTS):
            for d in range(2):
                ag_copy(st, d, 1, q).start()
        for q in range(CUTS):
            pf_copy(st, 0, q).start()

    def ag_event(st, hop, q):
        for d in range(2):
            if hop <= hops[d]:
                ag_copy(st, d, hop, q).wait_recv()
                if hop < hops[d]:
                    ag_copy(st, d, hop + 1, q).start()
                pf_copy(st, slot(d, hop), q).start()

    def total(st, s, received, q):
        value = x[st, place[s], 0, some(q), values].astype(jnp.float32)
        value = value + pc[st, s, some(q)].astype(jnp.float32)
        for index in received:
            value = value + rs[st, index, some(q)].astype(jnp.float32)
        return value.astype(jnp.bfloat16)

    def rs_event(st, age, q):
        for d in range(2):
            hop = hops[d] - age
            if hop >= 1:
                s = slot(d, hop)
                received = []
                if age:
                    rs_copy(st, d, hop + 1, q).wait_recv()
                    received = [s]
                if q == 0:
                    pc_copy(st, mirror(s)).wait_recv()
                x[st, place[s], 0, some(q), values] = total(st, s, received, q)
                rs_copy(st, d, hop, q).start()

    def rs_close(st, q):
        if q == 0:
            pc_copy(st, 0).wait_recv()
        for d in range(2):
            rs_copy(st, d, 1, q).wait_recv()
        out_ref[st, some(q)] = total(st, 0, [0, chips // 2], q)

    group = chips // 2
    block = min(4, group)
    tall = block * 2 * rows
    ff_tile = 256 if inner % 256 == 0 else inner
    out_tile = 512 if width % 512 == 0 else width

    def over_blocks(first, body):
        if group == block:
            body(first, 0)
        else:
            def step(i, carry):
                body(first + i * block, i * tall)
                return carry

            lax.fori_loop(0, group // block, step, 0)

    def gate_up(st, part, tile):
        columns = pl.ds(tile * ff_tile, ff_tile)

        def body(first, row):
            rows_in = x[st, pl.ds(first, block), :, :, values].reshape(tall, width)
            g = jnp.dot(rows_in, gate[:, columns], preferred_element_type=jnp.float32)
            u = jnp.dot(rows_in, up[:, columns], preferred_element_type=jnp.float32)
            mid[pl.ds(row, tall), columns] = (g / (1.0 + jnp.exp(-g)) * u).astype(jnp.bfloat16)

        over_blocks(part * group, body)

    def down_all(st, part):
        for s in order[part * group : (part + 1) * group]:
            for q in range(CUTS):
                pf_copy(st, s, q).wait_send()
                for d in range(2):
                    for hop in range(hops[d]):
                        if slot(d, hop) == s:
                            ag_copy(st, d, hop + 1, q).wait_send()

        def body(first, row):
            marks = x[st, pl.ds(first, block), :, :, pl.ds(width, extra)].reshape(tall, extra)
            spot = lax.broadcasted_iota(jnp.int32, (tall, extra), 1)
            picked = (spot == me) | (spot == me + experts)
            scale = jnp.sum(
                jnp.where(picked, marks.astype(jnp.float32), 0.0), axis=1, keepdims=True
            )
            rows_in = mid[pl.ds(row, tall), :]

            def tile(i, carry):
                columns = pl.ds(pl.multiple_of(i * out_tile, out_tile), out_tile)
                y = jnp.dot(rows_in, down[:, columns], preferred_element_type=jnp.float32)
                y = (y * scale).astype(jnp.bfloat16).reshape(block, 2, rows, out_tile)
                x[st, pl.ds(first, block), :, :, columns] = y
                return carry

            lax.fori_loop(0, width // out_tile, tile, 0)

        over_blocks(part * group, body)
        for s in order[part * group : (part + 1) * group]:
            pc_copy(st, s).start()

    def arrive(st, part):
        for s in order[part * group : (part + 1) * group]:
            for q in range(CUTS):
                pf_copy(st, mirror(s), q).wait_recv()

    def compute(st, part, events):
        tiles = inner // ff_tile
        pieces = tiles + 1
        arrive(st, part)
        taken = 0
        for piece in range(pieces):
            if piece < tiles:
                gate_up(st, part, piece)
            else:
                down_all(st, part)
            until = (piece + 1) * len(events) // pieces
            for event in events[taken:until]:
                event()
            taken = until

    near = group // 2
    call = functools.partial

    def gathers(st, first, last):
        return [
            call(ag_event, st, hop, q) for hop in range(first, last + 1) for q in range(CUTS)
        ]

    def returns(st, first, last):
        return [call(rs_event, st, age, q) for age in range(first, last) for q in range(CUTS)]

    far = hops[0]
    first, second = gathers(0, near + 1, far), gathers(1, 1, far)
    half = len(first) // 2
    ag_open(0)
    for event in gathers(0, 1, near):
        event()
    ag_open(1)
    for copy in loads:
        copy.wait()
    compute(0, 0, first[:half] + second[:half] + first[half:])
    compute(0, 1, second[half : 3 * half])
    middle = max(1, far // 2)
    for event in returns(0, 0, 1):
        event()
    compute(1, 0, second[3 * half :] + returns(0, 1, middle))
    compute(1, 1, returns(0, middle, far - 1))
    closing = [call(rs_close, 0, q) for q in range(CUTS)]
    for event in returns(1, 0, 1) + returns(0, far - 1, far) + returns(1, 1, 2):
        event()
    for event in closing + returns(1, 2, far):
        event()
    for q in range(CUTS):
        rs_close(1, q)

    for st in range(steps):
        for d in range(2):
            for hop in range(1, hops[d] + 1):
                for q in range(CUTS):
                    rs_copy(st, d, hop, q).wait_send()
        for s in range(chips):
            pc_copy(st, s).wait_send()


def on_device(across, hidden_states, route_ids, route_weights, gate_proj, up_proj, down_proj):
    steps, rows, width = hidden_states.shape
    experts = lax.axis_size("expert")
    inner = gate_proj.shape[2]
    chips = experts // 2
    hops = chips // 2
    extra = -(-2 * experts // LANES) * LANES
    dma = pltpu.SemaphoreType.DMA
    bf16 = jnp.bfloat16
    vmem = pl.BlockSpec(memory_space=pltpu.VMEM)
    hbm = pl.BlockSpec(memory_space=pl.ANY)
    return pl.pallas_call(
        functools.partial(kernel, chips, across),
        out_shape=jax.ShapeDtypeStruct((steps, rows, width), bf16),
        in_specs=[hbm, vmem, vmem, hbm, hbm, hbm],
        out_specs=vmem,
        scratch_shapes=[
            pltpu.VMEM((steps, chips, 2, rows, width + extra), bf16),
            pltpu.VMEM((steps, chips, rows, width), bf16),
            pltpu.VMEM((steps, chips, rows, width), bf16),
            pltpu.VMEM((width, inner), bf16),
            pltpu.VMEM((width, inner), bf16),
            pltpu.VMEM((inner, width), bf16),
            pltpu.VMEM((chips * rows, inner), bf16),
            dma((3 + steps,)),
            dma((steps, 2, hops, CUTS)),
            dma((steps, 2, hops, CUTS)),
            dma((steps, chips, CUTS)),
            dma((steps, chips, CUTS)),
            dma((steps, chips)),
            dma((steps, chips)),
            dma((steps, 2, hops, CUTS)),
            dma((steps, 2, hops, CUTS)),
        ],
        compiler_params=pltpu.CompilerParams(
            collective_id=0, has_side_effects=True, vmem_limit_bytes=64_000_000
        ),
    )(hidden_states, route_ids.swapaxes(1, 2), route_weights.swapaxes(1, 2), gate_proj, up_proj, down_proj)


def solution(mesh):
    across = 2 if mesh.shape["groups"] == 2 else 1
    placed = (
        P(None, ("groups", "expert"), None),
        P(None, ("groups", "expert"), None),
        P(None, ("groups", "expert"), None),
        P("expert", None, None),
        P("expert", None, None),
        P("expert", None, None),
    )
    return jax.shard_map(
        functools.partial(on_device, across),
        mesh=mesh,
        in_specs=placed,
        out_specs=P(None, ("groups", "expert"), None),
        check_vma=False,
    )
```

profile of v0, /device:TPU:0, one launch (start us, length us, event | category | flops | bytes accessed | tf_op | source)
XLA Modules:
  0.0 71.2 jit_solution(4694384132354632934)
XLA Ops:
  0.0 69.5 %shard_map.64 = bf16[2,32,2560]{2,1,0:T(8,128)(2,1)} custom-call(bf16[2,32,2560]{2,1,0:T(8,128)(2,1)} %hidden_ref.1, s32[2,8,32]{2,1,0:T(8,128)} %bitcast.2, f32[2,8,32]{2,1,0:T(8,128)} %bitcast.3, bf16[1,2560,768]{2,1,0:T(8,128)(2,1)} %gate_hbm.1, bf16[1,2560,768]{2,1,0:T(8,128)(2,1)} %up_hbm.1, bf16[1,768,2560]{2,1,0:T(8,128)(2,1)} %down_hbm.1), custom_call_target="tpu_custom_call" | custom-call | tf_op jit(solution)/shard_map/pallas_call | solution.py:349
  69.5 1.7 %copy.8 = bf16[2,32,2560]{2,1,0:T(8,128)(2,1)} copy(bf16[2,32,2560]{2,1,0:T(8,128)(2,1)} %shard_map.64) | data formatting | bytes 655360
where the time goes:
time: 71.5 us; the launch traced here: 71.2 us
  Pallas kernels  69.5 us (97%)
  local copies, waits for them, and re-layouts  1.72 us (2%)
    pallas_call x1, Pallas kernels, on_device(): pl.pallas_call(functools.partial(kernel, chips, across), out_shape=jax.Sh...  69.5 us
    unnamed x1, local copies, waits for them, and re-layouts  1.72 us

commit v1 on v0

v1 whole, which is shorter than its diff:
```python
import functools
import itertools

import jax
import jax.numpy as jnp
from jax import lax
from jax.experimental import pallas as pl
from jax.experimental.pallas import tpu as pltpu
from jax.sharding import PartitionSpec as P

MESH = pl.DeviceIdType.MESH
LANES = 128
SIDES = 2
DOWNS = 5
PARTS = 2
HOP_US = 2.7
CHUNK_US = 0.9
PAIR_US = 1.5
BACK_US = 2.0
GATHER_US = 0.05
SUM_US = 0.15
GATE_UP_US = 0.5
DOWN_US = 0.4


import itertools, random
def reach(chips,d,q,S=2): return chips//2 if q//S==d else chips-1-chips//2
def slot_at(chips,d,hop): return hop if d==0 else (chips-hop)%chips
def slots_in_order(chips):
    order=[0]
    for hop in range(1,chips//2+1): order+=[s for s in dict.fromkeys((hop,chips-hop))]
    return order
DEF=dict(HOP=2.7,CHUNK=0.9,PAIR=1.5,BACK=2.0,AG=0.05,SUM=0.12,GU=0.34,DN=0.17,DOWNS=5,tiles=6,
         inj=0.2,inj_after=0,hold=0,rs_first=0,mm_gap=0.0,rs0_bias=0.0,S=2)
def plan(chips=8,steps=2,**kw):
    p=dict(DEF);p.update(kw); S=p['S']
    tiles=p['tiles'];D=p['DOWNS']
    order=slots_in_order(chips);per=chips//2
    part_of={s:i//per for i,s in enumerate(order)}
    chunks=range(2*S);ops=[];free=[0.,0.];due={};held={};now=0.
    busy=0.
    def send(key,d):
        start=max(now,free[d]);free[d]=start+p['CHUNK'];due[key]=free[d]+p['HOP']
    later=[(st,d,q) for st in range(1,steps) for q in chunks for d in range(2)]
    for q in chunks:
        for d in range(2):
            ops.append(("own",0,d,q));send(("ag",0,d,1,q),d)
    for st in range(steps):
        for q in chunks: held[st,0,q]=0.
    mm=[(st,pt,pc) for st in range(steps) for pt in range(2) for pc in range(tiles+S*D)]
    scaled={}
    wrs=[(st,d,h,q) for st in range(steps) for q in chunks for d in range(2) for h in range(reach(chips,d,q,S),0,-1)]
    wc=[(st,q) for st in range(steps) for q in chunks]
    agleft={st:sum(reach(chips,d,q,S)-1 for q in chunks for d in range(2)) for st in range(steps)}
    def part_time(st,part):
        last=0.
        for s in order[part*per:(part+1)*per]:
            for q in chunks:
                for key,ex in (((st,s,q),0.),((st,(chips-s)%chips,q),p['PAIR'])):
                    if key not in held: return None
                    last=max(last,held[key]+ex)
        return last
    def summed(st,s,q):
        a=(st,part_of[s],q%S);b=(st,part_of[(chips-s)%chips],q%S)
        if a not in scaled or b not in scaled: return None
        return max(scaled[a],scaled[b]+p['BACK'])
    while mm or wrs or wc or due:
        if agleft[0]<=p['inj_after']:
            for e in list(later):
                st,d,q=e
                if free[d]<=now+p['inj'] and not any(f[1]==d for f in later[:later.index(e)]):
                    later.remove(e);ops.append(("own",st,d,q));send(("ag",st,d,1,q),d)
        ready=[]
        for key,when in due.items():
            if key[0]=="ag": ready.append((when,key))
        for st,d,h,q in wrs:
            when=summed(st,slot_at(chips,d,h),q)
            if when is None: continue
            if h<reach(chips,d,q,S):
                if ("rs",st,d,h+1,q) not in due: continue
                when=max(when,due["rs",st,d,h+1,q])
            ready.append((when,("sum",st,d,h,q)))
        for st,q in wc:
            when=summed(st,0,q)
            if when is None or any(("rs",st,d,1,q) not in due for d in range(2)): continue
            ready.append((max([when]+[due["rs",st,d,1,q] for d in range(2)]),("close",st,q)))
        def prio(e):
            when,k=e
            cls={"ag":0,"sum":1 if not p['rs_first'] else -1,"close":5}[k[0]]
            if k[0]=="ag" and k[1]==1: cls+=0.5
            return (max(when,now),k[1],cls,when,-k[3] if len(k)>3 else 0)
        ready.sort(key=prio)
        comp=None
        if mm:
            st,pt,pc=mm[0]
            if not (st==0 and agleft[0]>p['hold']): comp=part_time(st,pt)
        dur=None
        if ready and ready[0][0]<=now: pick=ready[0][1]
        elif comp is not None and comp<=now and not (ready and ready[0][0]<now+p['mm_gap']): pick=("matmul",*mm.pop(0))
        else:
            times=[e[0] for e in ready]+([comp] if comp is not None and comp>now else [])
            if later and agleft[0]<=p['inj_after']: times.append(max(now,min(free[e[1]] for e in later)-p['inj'])+0.01)
            now=min(times);continue
        ops.append(pick)
        if pick[0]=="ag":
            _,st,d,h,q=pick;del due[pick];now+=p['AG'];held[st,slot_at(chips,d,h),q]=now
            if h<reach(chips,d,q,S): send(("ag",st,d,h+1,q),d);agleft[st]-=1
        elif pick[0]=="matmul":
            _,st,pt,pc=pick
            if pc<tiles: now+=p['GU']
            else:
                now+=p['DN'];scaled[st,pt,(pc-tiles)//D]=now
        elif pick[0]=="sum":
            _,st,d,h,q=pick;now+=p['SUM'];wrs.remove((st,d,h,q));due.pop(("rs",st,d,h+1,q),None);send(("rs",st,d,h,q),1-d)
        else:
            _,st,q=pick;now+=p['SUM'];wc.remove((st,q))
            for d in range(2): del due["rs",st,d,1,q]
    return ops,now

def kernel(
    chips,
    across,
    hidden_ref,
    ids_hbm,
    weights_hbm,
    gate_hbm,
    up_hbm,
    down_hbm,
    out_hbm,
    ids_ref,
    weights_ref,
    out,
    gate_sum,
    x,
    pc,
    rs,
    table,
    gate,
    up,
    down,
    mid,
    scale,
    load_sem,
    ag_s,
    ag_r,
    pf_s,
    pf_r,
    pc_s,
    pc_r,
    rs_s,
    rs_r,
    tb_s,
    tb_r,
    tp_s,
    tp_r,
    out_s,
):
    steps, _, _, rows, width = x.shape
    inner = gate.shape[1]
    experts = 2 * chips
    along = chips // across

    me = lax.axis_index("expert")
    core = lax.rem(me, 2)
    chip = lax.div(me, 2)
    if across == 2:
        far, deep = lax.rem(chip, 2), lax.div(chip, 2)
        here = (1 - far) * deep + far * (2 * along - 1 - deep)
    else:
        here = chip

    def device_at(position):
        if across == 2:
            far = lax.div(position, along)
            deep = (1 - far) * position + far * (2 * along - 1 - position)
            position = deep * 2 + far
        return {"expert": position * 2 + core}

    sign = 1 - 2 * core
    neighbours = (
        device_at(lax.rem(here + sign + chips, chips)),
        device_at(lax.rem(here - sign + chips, chips)),
    )
    partner = {"expert": chip * 2 + (1 - core)}
    slot = functools.partial(slot_at, chips)
    order = slots_in_order(chips)
    place = {s: i for i, s in enumerate(order)}
    per = chips // PARTS
    part_of = {s: i // per for i, s in enumerate(order)}
    high, wide = rows // 2, width // SIDES

    def mirror(s):
        return (chips - s) % chips

    def area(q):
        return pl.ds(q // SIDES * high, high), pl.ds(q % SIDES * wide, wide)

    def remote(src, dst, send, recv, target):
        return pltpu.make_async_remote_copy(
            src_ref=src,
            dst_ref=dst,
            send_sem=send,
            recv_sem=recv,
            device_id=target,
            device_id_type=MESH,
        )

    def ag_copy(st, d, hop, q):
        return remote(
            x.at[st, place[slot(d, hop - 1)], 0, *area(q)],
            x.at[st, place[slot(d, hop)], 0, *area(q)],
            ag_s.at[st, part_of[slot(d, hop - 1)]],
            ag_r.at[st, place[slot(d, hop)] - 1, q],
            neighbours[d],
        )

    def pf_copy(st, s, q):
        return remote(
            x.at[st, place[s], 0, *area(q)],
            x.at[st, place[mirror(s)], 1, *area(q)],
            pf_s.at[st, part_of[s]],
            pf_r.at[st, part_of[mirror(s)]],
            partner,
        )

    def pc_copy(st, s, c):
        columns = pl.ds(c * wide, wide)
        return remote(
            x.at[st, place[s], 1, :, columns],
            pc.at[st, mirror(s), :, columns],
            pc_s,
            pc_r.at[st, part_of[s], c],
            partner,
        )

    def rs_copy(st, d, hop, q):
        target = slot(d, hop - 1) if (d == 0 or hop > 1) else chips // 2
        return remote(
            x.at[st, place[slot(d, hop)], 0, *area(q)],
            rs.at[st, target, *area(q)],
            rs_s,
            rs_r.at[st, target, q],
            neighbours[1 - d],
        )

    def tb_copy(d, hop):
        return remote(
            table.at[place[slot(d, hop - 1)], 0],
            table.at[place[slot(d, hop)], 0],
            tb_s,
            tb_r.at[place[slot(d, hop)] - 1],
            neighbours[d],
        )

    def tp_copy(s):
        return remote(
            table.at[place[s], 0],
            table.at[place[mirror(s)], 1],
            tp_s,
            tp_r.at[part_of[mirror(s)]],
            partner,
        )

    barrier = pltpu.get_barrier_semaphore()
    for target in (*neighbours, partner):
        pl.semaphore_signal(barrier, inc=1, device_id=target, device_id_type=MESH)

    own = [
        pltpu.make_async_copy(hidden_ref.at[st], x.at[st, 0, 0], load_sem.at[3 + st])
        for st in range(steps)
    ]
    for copy in own:
        copy.start()
    loads = [
        pltpu.make_async_copy(src.at[0], dst, load_sem.at[i])
        for i, (src, dst) in enumerate(((gate_hbm, gate), (up_hbm, up), (down_hbm, down)))
    ]
    small = [
        pltpu.make_async_copy(src, dst, load_sem.at[3 + steps + i])
        for i, (src, dst) in enumerate(((ids_hbm, ids_ref), (weights_hbm, weights_ref)))
    ]
    for copy in small:
        copy.start()
    for copy in loads:
        copy.start()
    own[0].wait()
    pl.semaphore_wait(barrier, 3)

    lanes = table.shape[3]

    def table_open():
        for copy in small:
            copy.wait()
        label = lax.broadcasted_iota(jnp.int32, (experts, rows), 0)
        for st in range(steps):
            raw = weights_ref[st]
            normalized = raw / jnp.sum(raw, axis=0, keepdims=True)
            ids = ids_ref[st]
            dense = jnp.zeros((experts, rows), jnp.float32)
            for k in range(ids.shape[0]):
                dense = dense + jnp.where(label == ids[k : k + 1], normalized[k : k + 1], 0.0)
            table[0, 0, :, pl.ds(st * rows, rows)] = dense
        for d in range(2):
            tb_copy(d, 1).start()
        tp_copy(0).start()

    def table_event(d, hop):
        tb_copy(d, hop).wait_recv()
        if hop < reach(chips, d, 0):
            tb_copy(d, hop + 1).start()
        tp_copy(slot(d, hop)).start()

    def ag_event(st, d, hop, q):
        if st == 0 and q == 1 and hop <= reach(chips, d, 0):
            table_event(d, hop)
        ag_copy(st, d, hop, q).wait_recv()
        if hop < reach(chips, d, q):
            ag_copy(st, d, hop + 1, q).start()
        pf_copy(st, slot(d, hop), q).start()

    summed = set()

    def partner_sums(st, s, c):
        key = (st, part_of[mirror(s)], c)
        if key not in summed:
            summed.add(key)
            some = pc.at[st, pl.ds(0, per), :, pl.ds(c * wide, wide)]
            pltpu.make_async_copy(some, some, pc_r.at[key]).wait()

    def total(st, s, received, q):
        partner_sums(st, s, q % SIDES)
        value = x[st, place[s], 0, *area(q)].astype(jnp.float32)
        value = value + pc[st, s, *area(q)].astype(jnp.float32)
        for index in received:
            value = value + rs[st, index, *area(q)].astype(jnp.float32)
        return value.astype(jnp.bfloat16)

    def rs_event(st, d, hop, q):
        s = slot(d, hop)
        received = []
        if hop < reach(chips, d, q):
            rs_copy(st, d, hop + 1, q).wait_recv()
            received = [s]
        x[st, place[s], 0, *area(q)] = total(st, s, received, q)
        rs_copy(st, d, hop, q).start()

    def out_copy(st, q):
        return pltpu.make_async_copy(out.at[st, *area(q)], out_hbm.at[st, *area(q)], out_s)

    def rs_close(st, q):
        for d in range(2):
            rs_copy(st, d, 1, q).wait_recv()
        out[st, *area(q)] = total(st, 0, [0, chips // 2], q)
        out_copy(st, q).start()

    block = min(4, per)
    tall = block * 2 * rows
    ff_tile = 256 if inner % 256 == 0 else inner
    tiles = 2 * inner // ff_tile

    def over_blocks(first, body):
        if per == block:
            body(first, 0)
        else:
            def step(i, carry):
                body(first + i * block, i * tall)
                return carry

            lax.fori_loop(0, per // block, step, 0)

    def gate_up(st, part, tile):
        columns = pl.ds(tile // 2 * ff_tile, ff_tile)

        def body(first, row):
            rows_in = x[st, pl.ds(first, block)].reshape(tall, width)
            if tile % 2 == 0:
                g = jnp.dot(rows_in, gate[:, columns], preferred_element_type=jnp.float32)
                gate_sum[pl.ds(row, tall)] = g / (1.0 + jnp.exp(-g))
            else:
                u = jnp.dot(rows_in, up[:, columns], preferred_element_type=jnp.float32)
                mid[pl.ds(row, tall), columns] = (gate_sum[pl.ds(row, tall)] * u).astype(jnp.bfloat16)

        over_blocks(part * per, body)

    def fill_scale(st, part):
        if st == 0:
            some = table.at[pl.ds(0, per), 0]
            pltpu.make_async_copy(some, some, tp_r.at[part]).wait()
        spot = lax.broadcasted_iota(jnp.int32, (experts, lanes), 0)
        blocks = 2 * block
        column = lax.broadcasted_iota(jnp.int32, (tall, blocks), 1)
        group = lax.broadcasted_iota(jnp.int32, (tall, blocks), 0) // rows

        def body(first, row):
            picked = [
                jnp.sum(jnp.where(spot == me, table[first + i, c], 0.0), axis=0, keepdims=True)
                for i in range(block)
                for c in range(2)
            ]
            turned = jnp.concatenate(picked, axis=0).T[st * rows : (st + 1) * rows]
            spread = jnp.concatenate([turned] * blocks, axis=0)
            weight = jnp.sum(jnp.where(column == group, spread, 0.0), axis=1, keepdims=True)
            scale[pl.ds(row, tall), :] = jnp.broadcast_to(weight, (tall, LANES))

        over_blocks(part * per, body)

    def down_part(st, part, piece):
        c, third = piece // DOWNS, piece % DOWNS
        if piece == 0:
            fill_scale(st, part)
            onward = sum(
                hop < reach(chips, d, q)
                for d in range(2)
                for q in range(2 * SIDES)
                for hop in range(reach(chips, d, q))
                if part_of[slot(d, hop)] == part
            )
            for blocks, sem in ((onward // (2 * SIDES), ag_s), (per, pf_s)):
                some = x.at[st, pl.ds(0, blocks), 0]
                pltpu.make_async_copy(some, some, sem.at[st, part]).wait()
        start, stop = (wide // LANES * (third + i) // DOWNS * LANES for i in range(2))
        columns = pl.ds(c * wide + start, stop - start)

        def body(first, row):
            v = jnp.dot(
                mid[pl.ds(row, tall), :], down[:, columns], preferred_element_type=jnp.float32
            )
            weight = scale[pl.ds(row, tall), :]
            v = v * jnp.concatenate([weight] * ((stop - start) // LANES), axis=1)
            v = v.astype(jnp.bfloat16).reshape(block, 2, rows, stop - start)
            x[st, pl.ds(first, block), :, :, columns] = v

        over_blocks(part * per, body)
        if third == DOWNS - 1:
            for s in order[part * per : (part + 1) * per]:
                pc_copy(st, s, c).start()

    arrived = set()
    loaded = set()

    def matmul_event(st, part, piece):
        if (st, part) not in arrived:
            arrived.add((st, part))
            some = x.at[st, pl.ds(0, per), 1]
            pltpu.make_async_copy(some, some, pf_r.at[st, part]).wait()
        if not loaded:
            loaded.add(0)
            for copy in loads:
                copy.wait()
        if piece < tiles:
            gate_up(st, part, piece)
        else:
            down_part(st, part, piece - tiles)

    def own_event(st, d, q):
        if q == 0 and d == 0 and st > 0:
            own[st].wait()
        ag_copy(st, d, 1, q).start()
        if q == SIDES * 2 - 1 and d == 1:
            for c in range(2 * SIDES):
                pf_copy(st, 0, c).start()
            if st == 0:
                table_open()

    run = {
        "own": own_event,
        "ag": ag_event,
        "matmul": matmul_event,
        "sum": rs_event,
        "close": rs_close,
    }
    for name, *where in plan(chips, steps, tiles=tiles, DOWNS=DOWNS, inj=2.0, inj_after=4, mm_gap=0.2, HOP=2.5)[0]:
        run[name](*where)

    for sent, sem in (
        (x.at[:, :, 1], pc_s),
        (x.at[:, pl.ds(0, chips - 1), 0], rs_s),
        (table.at[pl.ds(0, chips - 1), 0], tb_s),
        (table.at[:, 0], tp_s),
        (out, out_s),
    ):
        pltpu.make_async_copy(sent, sent, sem).wait()


def on_device(across, hidden_states, route_ids, route_weights, gate_proj, up_proj, down_proj):
    steps, rows, width = hidden_states.shape
    experts = lax.axis_size("expert")
    inner = gate_proj.shape[2]
    chips = experts // 2
    per = chips // PARTS
    lanes = -(-steps * rows // LANES) * LANES
    dma = pltpu.SemaphoreType.DMA
    bf16 = jnp.bfloat16
    hbm = pl.BlockSpec(memory_space=pl.ANY)
    return pl.pallas_call(
        functools.partial(kernel, chips, across),
        out_shape=jax.ShapeDtypeStruct((steps, rows, width), bf16),
        in_specs=[hbm] * 6,
        out_specs=hbm,
        scratch_shapes=[
            pltpu.VMEM((steps, route_ids.shape[2], rows), jnp.int32),
            pltpu.VMEM((steps, route_ids.shape[2], rows), jnp.float32),
            pltpu.VMEM((steps, rows, width), bf16),
            pltpu.VMEM((per * 2 * rows, 256 if inner % 256 == 0 else inner), jnp.float32),
            pltpu.VMEM((steps, chips, 2, rows, width), bf16),
            pltpu.VMEM((steps, chips, rows, width), bf16),
            pltpu.VMEM((steps, chips, rows, width), bf16),
            pltpu.VMEM((chips, 2, experts, lanes), jnp.float32),
            pltpu.VMEM((width, inner), bf16),
            pltpu.VMEM((width, inner), bf16),
            pltpu.VMEM((inner, width), bf16),
            pltpu.VMEM((per * 2 * rows, inner), bf16),
            pltpu.VMEM((per * 2 * rows, LANES), jnp.float32),
            dma((5 + steps,)),
            dma((steps, PARTS)),
            dma((steps, chips - 1, 2 * SIDES)),
            dma((steps, PARTS)),
            dma((steps, PARTS)),
            dma,
            dma((steps, PARTS, SIDES)),
            dma,
            dma((steps, chips, 2 * SIDES)),
            dma,
            dma((chips - 1,)),
            dma,
            dma((PARTS,)),
            dma,
        ],
        compiler_params=pltpu.CompilerParams(
            collective_id=0, has_side_effects=True, vmem_limit_bytes=64_000_000
        ),
    )(hidden_states, route_ids.swapaxes(1, 2), route_weights.swapaxes(1, 2), gate_proj, up_proj, down_proj)


def solution(mesh):
    across = 2 if mesh.shape["groups"] == 2 else 1
    placed = (
        P(None, ("groups", "expert"), None),
        P(None, ("groups", "expert"), None),
        P(None, ("groups", "expert"), None),
        P("expert", None, None),
        P("expert", None, None),
        P("expert", None, None),
    )
    return jax.shard_map(
        functools.partial(on_device, across),
        mesh=mesh,
        in_specs=placed,
        out_specs=P(None, ("groups", "expert"), None),
        check_vma=False,
    )
```

time: 71.5 us -> 64.8 us (0.906)
  Pallas kernels: 69.5 us -> 62.9 us
    pallas_call x1, Pallas kernels: 69.5 us -> 62.9 us  [on_device(): pl.pallas_call(functools.partial(kernel, chips, across), out_shape=jax.Sh...]
where the time goes in v1:
time: 64.8 us; the launch traced here: 64.6 us
  Pallas kernels  62.9 us (97%)
  local copies, waits for them, and re-layouts  1.72 us (3%)
    pallas_call x1, Pallas kernels, on_device(): pl.pallas_call(functools.partial(kernel, chips, across), out_shape=jax.Sh...  62.9 us
    unnamed x1, local copies, waits for them, and re-layouts  1.72 us

profile of v1, /device:TPU:0, one launch (start us, length us, event | category | flops | bytes accessed | tf_op | source)
XLA Modules:
  0.0 64.6 jit_solution(16590147886521347449)
XLA Ops:
  0.0 62.9 %shard_map.64 = bf16[2,32,2560]{2,1,0:T(8,128)(2,1)} custom-call(bf16[2,32,2560]{2,1,0:T(8,128)(2,1)} %hidden_ref.1, s32[2,8,32]{2,1,0:T(8,128)} %bitcast.2, f32[2,8,32]{2,1,0:T(8,128)} %bitcast.3, bf16[1,2560,768]{2,1,0:T(8,128)(2,1)} %gate_hbm.1, bf16[1,2560,768]{2,1,0:T(8,128)(2,1)} %up_hbm.1, bf16[1,768,2560]{2,1,0:T(8,128)(2,1)} %down_hbm.1), custom_call_target="tpu_custom_call" | custom-call | tf_op jit(solution)/shard_map/pallas_call | solution.py:495
  62.9 1.7 %copy.8 = bf16[2,32,2560]{2,1,0:T(8,128)(2,1)} copy(bf16[2,32,2560]{2,1,0:T(8,128)(2,1)} %shard_map.64) | data formatting | bytes 655360

commit v2 on v1

--- a/solution.py
+++ b/solution.py
@@ -126,10 +126,9 @@
     gate_hbm,
     up_hbm,
     down_hbm,
-    out_hbm,
+    out,
     ids_ref,
     weights_ref,
-    out,
     gate_sum,
     x,
     pc,
@@ -153,7 +152,6 @@
     tb_r,
     tp_s,
     tp_r,
-    out_s,
 ):
     steps, _, _, rows, width = x.shape
     inner = gate.shape[1]
@@ -286,7 +284,7 @@
     own[0].wait()
     pl.semaphore_wait(barrier, 3)
 
-    lanes = table.shape[3]
+    listed, lanes = table.shape[2:]
 
     def table_open():
         for copy in small:
@@ -299,7 +297,9 @@
             dense = jnp.zeros((experts, rows), jnp.float32)
             for k in range(ids.shape[0]):
                 dense = dense + jnp.where(label == ids[k : k + 1], normalized[k : k + 1], 0.0)
-            table[0, 0, :, pl.ds(st * rows, rows)] = dense
+            for g in range(experts // listed):
+                lane = (g * steps + st) * rows
+                table[0, 0, :, pl.ds(lane, rows)] = dense[g * listed : (g + 1) * listed]
         for d in range(2):
             tb_copy(d, 1).start()
         tp_copy(0).start()
@@ -344,14 +344,10 @@
         x[st, place[s], 0, *area(q)] = total(st, s, received, q)
         rs_copy(st, d, hop, q).start()
 
-    def out_copy(st, q):
-        return pltpu.make_async_copy(out.at[st, *area(q)], out_hbm.at[st, *area(q)], out_s)
-
     def rs_close(st, q):
         for d in range(2):
             rs_copy(st, d, 1, q).wait_recv()
         out[st, *area(q)] = total(st, 0, [0, chips // 2], q)
-        out_copy(st, q).start()
 
     block = min(4, per)
     tall = block * 2 * rows
@@ -386,19 +382,25 @@
         if st == 0:
             some = table.at[pl.ds(0, per), 0]
             pltpu.make_async_copy(some, some, tp_r.at[part]).wait()
-        spot = lax.broadcasted_iota(jnp.int32, (experts, lanes), 0)
+        spot = lax.broadcasted_iota(jnp.int32, (listed, lanes), 0)
+        mine, beside = lax.rem(me, listed), lax.div(me, listed)
         blocks = 2 * block
         column = lax.broadcasted_iota(jnp.int32, (tall, blocks), 1)
         group = lax.broadcasted_iota(jnp.int32, (tall, blocks), 0) // rows
 
         def body(first, row):
             picked = [
-                jnp.sum(jnp.where(spot == me, table[first + i, c], 0.0), axis=0, keepdims=True)
+                jnp.sum(jnp.where(spot == mine, table[first + i, c], 0.0), axis=0, keepdims=True)
                 for i in range(block)
                 for c in range(2)
             ]
-            turned = jnp.concatenate(picked, axis=0).T[st * rows : (st + 1) * rows]
-            spread = jnp.concatenate([turned] * blocks, axis=0)
+            turned = jnp.concatenate(picked, axis=0).T
+            own_rows = sum(
+                jnp.where(beside == g, turned[lane : lane + rows], 0.0)
+                for g in range(experts // listed)
+                for lane in ((g * steps + st) * rows,)
+            )
+            spread = jnp.concatenate([own_rows] * blocks, axis=0)
             weight = jnp.sum(jnp.where(column == group, spread, 0.0), axis=1, keepdims=True)
             scale[pl.ds(row, tall), :] = jnp.broadcast_to(weight, (tall, LANES))
 
@@ -469,7 +471,7 @@
         "sum": rs_event,
         "close": rs_close,
     }
-    for name, *where in plan(chips, steps, tiles=tiles, DOWNS=DOWNS, inj=2.0, inj_after=4, mm_gap=0.2, HOP=2.5)[0]:
+    for name, *where in plan(chips, steps, tiles=tiles, DOWNS=DOWNS, inj=2.0, inj_after=4, mm_gap=0.2, HOP=2.0)[0]:
         run[name](*where)
 
     for sent, sem in (
@@ -477,7 +479,6 @@
         (x.at[:, pl.ds(0, chips - 1), 0], rs_s),
         (table.at[pl.ds(0, chips - 1), 0], tb_s),
         (table.at[:, 0], tp_s),
-        (out, out_s),
     ):
         pltpu.make_async_copy(sent, sent, sem).wait()
 
@@ -488,24 +489,25 @@
     inner = gate_proj.shape[2]
     chips = experts // 2
     per = chips // PARTS
-    lanes = -(-steps * rows // LANES) * LANES
+    beside = max(1, LANES // (steps * rows))
+    beside = beside if experts % (8 * beside) == 0 else 1
+    lanes = -(-steps * rows * beside // LANES) * LANES
     dma = pltpu.SemaphoreType.DMA
     bf16 = jnp.bfloat16
     hbm = pl.BlockSpec(memory_space=pl.ANY)
     return pl.pallas_call(
         functools.partial(kernel, chips, across),
-        out_shape=jax.ShapeDtypeStruct((steps, rows, width), bf16),
+        out_shape=pltpu.VMEM((steps, rows, width), bf16),
         in_specs=[hbm] * 6,
-        out_specs=hbm,
+        out_specs=pl.BlockSpec(memory_space=pltpu.VMEM),
         scratch_shapes=[
             pltpu.VMEM((steps, route_ids.shape[2], rows), jnp.int32),
             pltpu.VMEM((steps, route_ids.shape[2], rows), jnp.float32),
-            pltpu.VMEM((steps, rows, width), bf16),
             pltpu.VMEM((per * 2 * rows, 256 if inner % 256 == 0 else inner), jnp.float32),
             pltpu.VMEM((steps, chips, 2, rows, width), bf16),
             pltpu.VMEM((steps, chips, rows, width), bf16),
             pltpu.VMEM((steps, chips, rows, width), bf16),
-            pltpu.VMEM((chips, 2, experts, lanes), jnp.float32),
+            pltpu.VMEM((chips, 2, experts // beside, lanes), jnp.float32),
             pltpu.VMEM((width, inner), bf16),
             pltpu.VMEM((width, inner), bf16),
             pltpu.VMEM((inner, width), bf16),
@@ -524,7 +526,6 @@
             dma((chips - 1,)),
             dma,
             dma((PARTS,)),
-            dma,
         ],
         compiler_params=pltpu.CompilerParams(
             collective_id=0, has_side_effects=True, vmem_limit_bytes=64_000_000

time: 64.8 us -> 62.8 us (0.969)
  local copies, waits for them, and re-layouts: 1.72 us -> 0.73 us
  Pallas kernels: 62.9 us -> 62 us
    unnamed x1, local copies, waits for them, and re-layouts: 1.72 us -> 0.73 us
    pallas_call x1, Pallas kernels: 62.9 us -> 62 us  [on_device(): pl.pallas_call(functools.partial(kernel, chips, across), out_shape=pltpu....]
where the time goes in v2:
time: 62.8 us; the launch traced here: 62.7 us
  Pallas kernels  62 us (99%)
  local copies, waits for them, and re-layouts  0.73 us (1%)
    pallas_call x1, Pallas kernels, on_device(): pl.pallas_call(functools.partial(kernel, chips, across), out_shape=pltpu....  62 us

profile of v2, /device:TPU:0, one launch (start us, length us, event | category | flops | bytes accessed | tf_op | source)
XLA Modules:
  0.0 62.7 jit_solution(11299584766195022825)
XLA Ops:
  0.0 62.0 %shard_map.64 = bf16[2,32,2560]{2,1,0:T(8,128)(2,1)S(1)} custom-call(bf16[2,32,2560]{2,1,0:T(8,128)(2,1)} %hidden_ref.1, s32[2,8,32]{2,1,0:T(8,128)} %bitcast.2, f32[2,8,32]{2,1,0:T(8,128)} %bitcast.3, bf16[1,2560,768]{2,1,0:T(8,128)(2,1)} %gate_hbm.1, bf16[1,2560,768]{2,1,0:T(8,128)(2,1)} %up_hbm.1, bf16[1,768,2560]{2,1,0:T(8,128)(2,1)} %down_hbm.1), custom_call_target="tpu_custom_call" | custom-call | tf_op jit(solution)/shard_map/pallas_call | solution.py:498
  62.0 0.7 %copy.8 = bf16[2,32,2560]{2,1,0:T(8,128)(2,1)} copy(bf16[2,32,2560]{2,1,0:T(8,128)(2,1)S(1)} %shard_map.64) | data formatting | bytes 655360

commit v3 on v2

--- a/solution.py
+++ b/solution.py
@@ -1,5 +1,4 @@
 import functools
-import itertools
 
 import jax
 import jax.numpy as jnp
@@ -13,109 +12,152 @@
 SIDES = 2
 DOWNS = 5
 PARTS = 2
-HOP_US = 2.7
+HOP_US = 1.6
 CHUNK_US = 0.9
 PAIR_US = 1.5
 BACK_US = 2.0
 GATHER_US = 0.05
-SUM_US = 0.15
-GATE_UP_US = 0.5
-DOWN_US = 0.4
-
-
-import itertools, random
-def reach(chips,d,q,S=2): return chips//2 if q//S==d else chips-1-chips//2
-def slot_at(chips,d,hop): return hop if d==0 else (chips-hop)%chips
+SUM_US = 0.12
+GATE_UP_US = 0.34
+DOWN_US = 0.17
+GAP_US = 0.2
+QUEUE_US = 2.0
+ONWARD = 4
+HOLD = 99
+
+
+def reach(chips, d, q):
+    return chips // 2 if q // SIDES == d else chips - 1 - chips // 2
+
+
+def slot_at(chips, d, hop):
+    return hop if d == 0 else (chips - hop) % chips
+
+
 def slots_in_order(chips):
-    order=[0]
-    for hop in range(1,chips//2+1): order+=[s for s in dict.fromkeys((hop,chips-hop))]
+    order = [0]
+    for hop in range(1, chips // 2 + 1):
+        order += dict.fromkeys((hop, chips - hop))
     return order
-DEF=dict(HOP=2.7,CHUNK=0.9,PAIR=1.5,BACK=2.0,AG=0.05,SUM=0.12,GU=0.34,DN=0.17,DOWNS=5,tiles=6,
-         inj=0.2,inj_after=0,hold=0,rs_first=0,mm_gap=0.0,rs0_bias=0.0,S=2)
-def plan(chips=8,steps=2,**kw):
-    p=dict(DEF);p.update(kw); S=p['S']
-    tiles=p['tiles'];D=p['DOWNS']
-    order=slots_in_order(chips);per=chips//2
-    part_of={s:i//per for i,s in enumerate(order)}
-    chunks=range(2*S);ops=[];free=[0.,0.];due={};held={};now=0.
-    busy=0.
-    def send(key,d):
-        start=max(now,free[d]);free[d]=start+p['CHUNK'];due[key]=free[d]+p['HOP']
-    later=[(st,d,q) for st in range(1,steps) for q in chunks for d in range(2)]
-    for q in chunks:
-        for d in range(2):
-            ops.append(("own",0,d,q));send(("ag",0,d,1,q),d)
+
+
+def plan(chips, steps, tiles):
+    order = slots_in_order(chips)
+    per = chips // PARTS
+    part_of = {s: i // per for i, s in enumerate(order)}
+    chunks = range(2 * SIDES)
+    ops, free, due, held, scaled, now = [], [0.0, 0.0], {}, {}, {}, 0.0
+    hops = [(d, q, reach(chips, d, q)) for q in chunks for d in range(2)]
+    own = [(st, d, q) for st in range(1, steps) for q in chunks for d in range(2)]
+    matmuls = [
+        (st, part, piece)
+        for st in range(steps)
+        for part in range(PARTS)
+        for piece in range(tiles + SIDES * DOWNS)
+    ]
+    sums = [(st, d, hop, q) for st in range(steps) for d, q, far in hops for hop in range(far, 0, -1)]
+    closes = [(st, q) for st in range(steps) for q in chunks]
+    onward = sum(far - 1 for _, _, far in hops)
+
+    def mirror(s):
+        return (chips - s) % chips
+
+    def send(key, d):
+        free[d] = max(now, free[d]) + CHUNK_US
+        due[key] = free[d] + HOP_US
+
+    def arrived(st, part):
+        times = []
+        for s in order[part * per : (part + 1) * per]:
+            for q in chunks:
+                if (st, s, q) not in held or (st, mirror(s), q) not in held:
+                    return None
+                times += [held[st, s, q], held[st, mirror(s), q] + PAIR_US]
+        return max(times)
+
+    def returned(st, s, q):
+        mine, theirs = (st, part_of[s], q % SIDES), (st, part_of[mirror(s)], q % SIDES)
+        if mine not in scaled or theirs not in scaled:
+            return None
+        return max(scaled[mine], scaled[theirs] + BACK_US)
+
+    def rank(event):
+        when, key = event
+        later = {"ag": key[1] * 0.5, "sum": 1, "close": 5}[key[0]]
+        return max(when, now), key[1], later, when, -key[3] if len(key) > 3 else 0
+
+    for d, q, _ in hops:
+        ops.append(("own", 0, d, q))
+        send(("ag", 0, d, 1, q), d)
     for st in range(steps):
-        for q in chunks: held[st,0,q]=0.
-    mm=[(st,pt,pc) for st in range(steps) for pt in range(2) for pc in range(tiles+S*D)]
-    scaled={}
-    wrs=[(st,d,h,q) for st in range(steps) for q in chunks for d in range(2) for h in range(reach(chips,d,q,S),0,-1)]
-    wc=[(st,q) for st in range(steps) for q in chunks]
-    agleft={st:sum(reach(chips,d,q,S)-1 for q in chunks for d in range(2)) for st in range(steps)}
-    def part_time(st,part):
-        last=0.
-        for s in order[part*per:(part+1)*per]:
-            for q in chunks:
-                for key,ex in (((st,s,q),0.),((st,(chips-s)%chips,q),p['PAIR'])):
-                    if key not in held: return None
-                    last=max(last,held[key]+ex)
-        return last
-    def summed(st,s,q):
-        a=(st,part_of[s],q%S);b=(st,part_of[(chips-s)%chips],q%S)
-        if a not in scaled or b not in scaled: return None
-        return max(scaled[a],scaled[b]+p['BACK'])
-    while mm or wrs or wc or due:
-        if agleft[0]<=p['inj_after']:
-            for e in list(later):
-                st,d,q=e
-                if free[d]<=now+p['inj'] and not any(f[1]==d for f in later[:later.index(e)]):
-                    later.remove(e);ops.append(("own",st,d,q));send(("ag",st,d,1,q),d)
-        ready=[]
-        for key,when in due.items():
-            if key[0]=="ag": ready.append((when,key))
-        for st,d,h,q in wrs:
-            when=summed(st,slot_at(chips,d,h),q)
-            if when is None: continue
-            if h<reach(chips,d,q,S):
-                if ("rs",st,d,h+1,q) not in due: continue
-                when=max(when,due["rs",st,d,h+1,q])
-            ready.append((when,("sum",st,d,h,q)))
-        for st,q in wc:
-            when=summed(st,0,q)
-            if when is None or any(("rs",st,d,1,q) not in due for d in range(2)): continue
-            ready.append((max([when]+[due["rs",st,d,1,q] for d in range(2)]),("close",st,q)))
-        def prio(e):
-            when,k=e
-            cls={"ag":0,"sum":1 if not p['rs_first'] else -1,"close":5}[k[0]]
-            if k[0]=="ag" and k[1]==1: cls+=0.5
-            return (max(when,now),k[1],cls,when,-k[3] if len(k)>3 else 0)
-        ready.sort(key=prio)
-        comp=None
-        if mm:
-            st,pt,pc=mm[0]
-            if not (st==0 and agleft[0]>p['hold']): comp=part_time(st,pt)
-        dur=None
-        if ready and ready[0][0]<=now: pick=ready[0][1]
-        elif comp is not None and comp<=now and not (ready and ready[0][0]<now+p['mm_gap']): pick=("matmul",*mm.pop(0))
+        held.update({(st, 0, q): 0.0 for q in chunks})
+
+    while matmuls or sums or closes or due:
+        if onward <= ONWARD:
+            for st, d, q in list(own):
+                first = next(entry for entry in own if entry[1] == d) == (st, d, q)
+                if first and free[d] <= now + QUEUE_US:
+                    own.remove((st, d, q))
+                    ops.append(("own", st, d, q))
+                    send(("ag", st, d, 1, q), d)
+        ready = [(when, key) for key, when in due.items() if key[0] == "ag"]
+        for st, d, hop, q in sums:
+            when = returned(st, slot_at(chips, d, hop), q)
+            before = ("rs", st, d, hop + 1, q)
+            if when is None or (hop < reach(chips, d, q) and before not in due):
+                continue
+            ready.append((max(when, due.get(before, 0.0)), ("sum", st, d, hop, q)))
+        for st, q in closes:
+            when = returned(st, 0, q)
+            last = [due.get(("rs", st, d, 1, q)) for d in range(2)]
+            if when is not None and None not in last:
+                ready.append((max(when, *last), ("close", st, q)))
+        ready.sort(key=rank)
+        start = None
+        if matmuls and (matmuls[0][0] > 0 or onward <= HOLD):
+            start = arrived(*matmuls[0][:2])
+        if ready and ready[0][0] <= now:
+            pick = ready[0][1]
+        elif start is not None and start <= now and not (ready and ready[0][0] < now + GAP_US):
+            pick = ("matmul", *matmuls.pop(0))
         else:
-            times=[e[0] for e in ready]+([comp] if comp is not None and comp>now else [])
-            if later and agleft[0]<=p['inj_after']: times.append(max(now,min(free[e[1]] for e in later)-p['inj'])+0.01)
-            now=min(times);continue
+            times = [when for when, _ in ready]
+            if start is not None and start > now:
+                times.append(start)
+            if own and onward <= ONWARD:
+                times.append(max(now, min(free[d] for _, d, _ in own) - QUEUE_US) + 0.01)
+            now = min(times)
+            continue
         ops.append(pick)
-        if pick[0]=="ag":
-            _,st,d,h,q=pick;del due[pick];now+=p['AG'];held[st,slot_at(chips,d,h),q]=now
-            if h<reach(chips,d,q,S): send(("ag",st,d,h+1,q),d);agleft[st]-=1
-        elif pick[0]=="matmul":
-            _,st,pt,pc=pick
-            if pc<tiles: now+=p['GU']
+        kind, st, *rest = pick
+        if kind == "ag":
+            d, hop, q = rest
+            del due[pick]
+            now += GATHER_US
+            held[st, slot_at(chips, d, hop), q] = now
+            if hop < reach(chips, d, q):
+                send(("ag", st, d, hop + 1, q), d)
+                onward -= st == 0
+        elif kind == "matmul":
+            part, piece = rest
+            if piece < tiles:
+                now += GATE_UP_US
             else:
-                now+=p['DN'];scaled[st,pt,(pc-tiles)//D]=now
-        elif pick[0]=="sum":
-            _,st,d,h,q=pick;now+=p['SUM'];wrs.remove((st,d,h,q));due.pop(("rs",st,d,h+1,q),None);send(("rs",st,d,h,q),1-d)
+                now += DOWN_US
+                scaled[st, part, (piece - tiles) // DOWNS] = now
+        elif kind == "sum":
+            d, hop, q = rest
+            now += SUM_US
+            sums.remove((st, d, hop, q))
+            due.pop(("rs", st, d, hop + 1, q), None)
+            send(("rs", st, d, hop, q), 1 - d)
         else:
-            _,st,q=pick;now+=p['SUM'];wc.remove((st,q))
-            for d in range(2): del due["rs",st,d,1,q]
-    return ops,now
+            now += SUM_US
+            closes.remove((st, *rest))
+            for d in range(2):
+                del due["rs", st, d, 1, *rest]
+    return ops
+
 
 def kernel(
     chips,
@@ -281,7 +323,6 @@
         copy.start()
     for copy in loads:
         copy.start()
-    own[0].wait()
     pl.semaphore_wait(barrier, 3)
 
     listed, lanes = table.shape[2:]
@@ -454,8 +495,11 @@
         else:
             down_part(st, part, piece - tiles)
 
+    begun = set()
+
     def own_event(st, d, q):
-        if q == 0 and d == 0 and st > 0:
+        if st not in begun:
+            begun.add(st)
             own[st].wait()
         ag_copy(st, d, 1, q).start()
         if q == SIDES * 2 - 1 and d == 1:
@@ -471,7 +515,7 @@
         "sum": rs_event,
         "close": rs_close,
     }
-    for name, *where in plan(chips, steps, tiles=tiles, DOWNS=DOWNS, inj=2.0, inj_after=4, mm_gap=0.2, HOP=2.0)[0]:
+    for name, *where in plan(chips, steps, tiles):
         run[name](*where)
 
     for sent, sem in (

time: 62.8 us -> 62.1 us (0.989)
  Pallas kernels: 62 us -> 61.2 us
    pallas_call x1, Pallas kernels: 62 us -> 61.2 us  [on_device(): pl.pallas_call(functools.partial(kernel, chips, across), out_shape=pltpu....]
where the time goes in v3:
time: 62.1 us; the launch traced here: 61.9 us
  Pallas kernels  61.2 us (99%)
  local copies, waits for them, and re-layouts  0.73 us (1%)
    pallas_call x1, Pallas kernels, on_device(): pl.pallas_call(functools.partial(kernel, chips, across), out_shape=pltpu....  61.2 us

profile of v3, /device:TPU:0, one launch (start us, length us, event | category | flops | bytes accessed | tf_op | source)
XLA Modules:
  0.0 61.9 jit_solution(8269716898169033858)
XLA Ops:
  0.0 61.2 %shard_map.64 = bf16[2,32,2560]{2,1,0:T(8,128)(2,1)S(1)} custom-call(bf16[2,32,2560]{2,1,0:T(8,128)(2,1)} %hidden_ref.1, s32[2,8,32]{2,1,0:T(8,128)} %bitcast.2, f32[2,8,32]{2,1,0:T(8,128)} %bitcast.3, bf16[1,2560,768]{2,1,0:T(8,128)(2,1)} %gate_hbm.1, bf16[1,2560,768]{2,1,0:T(8,128)(2,1)} %up_hbm.1, bf16[1,768,2560]{2,1,0:T(8,128)(2,1)} %down_hbm.1), custom_call_target="tpu_custom_call" | custom-call | tf_op jit(solution)/shard_map/pallas_call | solution.py:542
  61.2 0.7 %copy.8 = bf16[2,32,2560]{2,1,0:T(8,128)(2,1)} copy(bf16[2,32,2560]{2,1,0:T(8,128)(2,1)S(1)} %shard_map.64) | data formatting | bytes 655360

commit v4 on v3

--- a/solution.py
+++ b/solution.py
@@ -22,7 +22,7 @@
 DOWN_US = 0.17
 GAP_US = 0.2
 QUEUE_US = 2.0
-ONWARD = 4
+ONWARD = 2
 HOLD = 99
 
 

time: 62.1 us -> 62.9 us (1.013)
  Pallas kernels: 61.2 us -> 62.1 us
    pallas_call x1, Pallas kernels: 61.2 us -> 62.1 us  [on_device(): pl.pallas_call(functools.partial(kernel, chips, across), out_shape=pltpu....]
where the time goes in v4:
time: 62.9 us; the launch traced here: 62.8 us
  Pallas kernels  62.1 us (99%)
  local copies, waits for them, and re-layouts  0.73 us (1%)
    pallas_call x1, Pallas kernels, on_device(): pl.pallas_call(functools.partial(kernel, chips, across), out_shape=pltpu....  62.1 us

profile of v4, /device:TPU:0, one launch (start us, length us, event | category | flops | bytes accessed | tf_op | source)
XLA Modules:
  0.0 62.8 jit_solution(4052781145441798272)
XLA Ops:
  0.0 62.1 %shard_map.64 = bf16[2,32,2560]{2,1,0:T(8,128)(2,1)S(1)} custom-call(bf16[2,32,2560]{2,1,0:T(8,128)(2,1)} %hidden_ref.1, s32[2,8,32]{2,1,0:T(8,128)} %bitcast.2, f32[2,8,32]{2,1,0:T(8,128)} %bitcast.3, bf16[1,2560,768]{2,1,0:T(8,128)(2,1)} %gate_hbm.1, bf16[1,2560,768]{2,1,0:T(8,128)(2,1)} %up_hbm.1, bf16[1,768,2560]{2,1,0:T(8,128)(2,1)} %down_hbm.1), custom_call_target="tpu_custom_call" | custom-call | tf_op jit(solution)/shard_map/pallas_call | solution.py:542
  62.1 0.7 %copy.8 = bf16[2,32,2560]{2,1,0:T(8,128)(2,1)} copy(bf16[2,32,2560]{2,1,0:T(8,128)(2,1)S(1)} %shard_map.64) | data formatting | bytes 655360
